TPU v7x, 32 devices: a whole 2x2x4 slice. The times are simulated.
32 devices in a mesh: grp: 2 (over core), seq: 8 (over z, y), fsdp: 2 (over x).
Axes of the slice: x: 2, y: 2, z: 4, core: 2. Of those that a mesh axis runs over, the one named last changes fastest.
Arguments:
- new_rows: bfloat16 [1024, 5120], P('seq'), may hold values from -6 to 6
- cache_keys: bfloat16 [4, 512, 3072], P(None, None, 'fsdp'), may hold values from -16 to 16
- cache_values: bfloat16 [4, 512, 3072], P(None, None, 'fsdp'), may hold values from -6 to 6
- cache_frames: int32 [3], replicated, may hold values from 0 to 3
- real_bank: bfloat16 [2, 1024, 5120], P(None, 'seq'), may hold values from -6 to 6
- real_pick: int32 [1024], P('seq'), may hold values from 0 to 1
- attn_weights: bfloat16 [2, 3, 5120, 3072], P('grp', None, 'seq', 'fsdp'), may hold values from -1 to 1
- out_weights: bfloat16 [2, 3072, 5120], P('grp', 'seq', 'fsdp'), may hold values from -0.109375 to 0.109375
- norm_gains: float32 [2, 5120], P('grp'), may hold values from 0.5 to 1.5
- head_in: bfloat16 [5120, 128], P('fsdp'), may hold values from -0.078125 to 0.078125
- head_out: float32 [128], replicated, may hold values from -0.5 to 0.5
Outputs:
- wo_grads: bfloat16 [2, 3072, 5120], P('grp', 'seq', 'fsdp')
- losses: bfloat16 [2], P('grp')
All inputs are finite; a program needn't handle non-finite values.
Results may differ from a plain program's by a relative error of at most 0.014.
The roundings to bfloat16 on the way count: a program that leaves them out, or rounds other values in their place, can miss the bound.
Values may be sent and summed in bfloat16 or wider, within the bound.
A program may use at most 192 MiB of HBM per device.

v0:
```python
import jax
import jax.numpy as jnp
from jax import lax
from jax.sharding import PartitionSpec as P

HD = 128


EPS = 1e-06
NEG = -1e30


def passed_along(value, axis, steps):
    count = lax.axis_size(axis)
    leading, last = (max(0, -steps), min(count, count - steps))
    return lax.ppermute(value, axis, [(source, source + steps) for source in range(leading, last)])


def attend(queries, key_set, value_set, allowed):
    head_size = queries.shape[-1]
    scores = jnp.einsum(
        "rhd,khd->hrk", queries, key_set, preferred_element_type=jnp.float32
    ) * head_size ** (-0.5)
    if allowed is not None:
        scores = jnp.where(allowed[None], scores, NEG)
    row_max = jnp.max(scores, axis=-1, keepdims=True)
    raised = jnp.exp(scores - row_max)
    weights = raised / jnp.sum(raised, axis=-1, keepdims=True)
    result = jnp.einsum(
        "hrk,khd->rhd", weights.astype(jnp.bfloat16), value_set, preferred_element_type=jnp.float32
    )
    return (result, weights)


def project(row_block, gain_vector, weight_set):
    lifted = row_block.astype(jnp.float32)
    inverse = lax.rsqrt(jnp.mean(lifted * lifted, axis=-1, keepdims=True) + EPS)
    normed = (lifted * inverse * gain_vector).astype(jnp.bfloat16)
    projected = jnp.einsum("rd,cde->cre", normed, weight_set, preferred_element_type=jnp.float32)
    return (projected.astype(jnp.bfloat16), lifted, inverse)


def unit_direction(unit_values, head_out, head_cols):
    _, gelu_back = jax.vjp(jax.nn.gelu, unit_values)
    unit_grad = gelu_back(jnp.broadcast_to(head_out, unit_values.shape))[0].astype(jnp.bfloat16)
    return jnp.einsum("ru,cu->rc", unit_grad, head_cols, preferred_element_type=jnp.float32)


def pick_rows(real_bank, real_pick):
    chosen = jnp.zeros(real_bank.shape[1:], real_bank.dtype)
    for entry in range(real_bank.shape[0]):
        chosen = jnp.where((real_pick == entry)[:, None], real_bank[entry], chosen)
    return chosen


def local(
    new_rows,
    cache_keys,
    cache_values,
    cache_frames,
    real_bank,
    real_pick,
    attn_weights,
    out_weights,
    norm_gains,
    head_in,
    head_out,
):
    is_gen = lax.axis_index("grp") == 0
    seq_at = lax.axis_index("seq")
    fsdp_at = lax.axis_index("fsdp")
    row_count = new_rows.shape[0]
    local_weights = attn_weights[0]
    local_out = out_weights[0]
    col_count = local_out.shape[1]
    heads_width = local_weights.shape[2]
    head_count = heads_width // HD
    gain_vector = norm_gains[0]
    full_weights = lax.all_gather(local_weights, "seq", axis=1, tiled=True)
    full_out = lax.all_gather(local_out, "seq", axis=0, tiled=True)
    real_rows = pick_rows(real_bank, real_pick)
    first_rows = jnp.where(is_gen, new_rows, real_rows)
    first_proj, _, _ = project(first_rows, gain_vector, full_weights)
    first_keys, first_values = (
        lax.all_gather(first_proj[1], "seq", axis=0, tiled=True),
        lax.all_gather(first_proj[2], "seq", axis=0, tiled=True),
    )
    key_count = first_keys.shape[0]
    frame_len = key_count // 2
    first_query = first_proj[0].reshape(row_count, head_count, HD)
    own_keys = first_keys.reshape(key_count, head_count, HD)
    own_values = first_values.reshape(key_count, head_count, HD)

    def generator_attend(operand):
        picked_keys = jnp.take(cache_keys, cache_frames, axis=0).reshape(-1, head_count, HD)
        picked_values = jnp.take(cache_values, cache_frames, axis=0).reshape(-1, head_count, HD)
        query_frame = (seq_at * row_count + jnp.arange(row_count)) // frame_len
        key_frame = jnp.arange(key_count) // frame_len
        allowed = jnp.concatenate(
            [
                jnp.ones((row_count, picked_keys.shape[0]), jnp.bool_),
                key_frame[None, :] <= query_frame[:, None],
            ],
            axis=1,
        )
        all_keys = jnp.concatenate([picked_keys, own_keys], axis=0)
        all_values = jnp.concatenate([picked_values, own_values], axis=0)
        return attend(first_query, all_keys, all_values, allowed)[0].astype(jnp.bfloat16)

    def critic_attend(operand):
        return attend(first_query, own_keys, own_values, None)[0].astype(jnp.bfloat16)

    first_heads = lax.cond(is_gen, generator_attend, critic_attend, 0).reshape(
        row_count, heads_width
    )
    first_all = lax.all_gather(first_heads, "fsdp", axis=1, tiled=True)
    start_col = fsdp_at * col_count
    first_cols = lax.dynamic_slice_in_dim(first_rows, start_col, col_count, 1).astype(jnp.float32)
    first_out = (
        first_cols + jnp.dot(first_all, full_out, preferred_element_type=jnp.float32)
    ).astype(jnp.bfloat16)
    real_units = jnp.dot(first_out, head_in, preferred_element_type=jnp.float32)
    whole_rows = lax.all_gather(first_out, "fsdp", axis=1, tiled=True)
    second_rows = passed_along(whole_rows, "grp", 1)
    second_proj, second_lifted, second_inverse = project(second_rows, gain_vector, full_weights)
    second_keys, second_values = (
        lax.all_gather(second_proj[1], "seq", axis=0, tiled=True),
        lax.all_gather(second_proj[2], "seq", axis=0, tiled=True),
    )
    keys_two = second_keys.reshape(key_count, head_count, HD)
    values_two = second_values.reshape(key_count, head_count, HD)
    query_two = second_proj[0].reshape(row_count, head_count, HD)
    second_result, second_weights = attend(query_two, keys_two, values_two, None)
    second_heads = second_result.astype(jnp.bfloat16).reshape(row_count, heads_width)
    second_all = lax.all_gather(second_heads, "fsdp", axis=1, tiled=True)
    second_cols = lax.dynamic_slice_in_dim(second_lifted, start_col, col_count, 1)
    second_out = (
        second_cols + jnp.dot(second_all, full_out, preferred_element_type=jnp.float32)
    ).astype(jnp.bfloat16)
    fake_units = jnp.dot(second_out, head_in, preferred_element_type=jnp.float32)
    real_units, fake_units = (
        lax.psum(real_units.astype(jnp.bfloat16), "fsdp").astype(jnp.float32),
        lax.psum(fake_units.astype(jnp.bfloat16), "fsdp").astype(jnp.float32),
    )
    real_part = jnp.sum(jax.nn.gelu(real_units) * head_out)
    fake_part = jnp.sum(jax.nn.gelu(fake_units) * head_out)
    real_score, fake_score = lax.psum((real_part, fake_part), "seq")
    margin = (real_score - fake_score) / (row_count * lax.axis_size("seq"))
    loss_pair = jnp.stack([jax.nn.softplus(margin), jax.nn.softplus(-margin)]).astype(jnp.bfloat16)
    real_dir = unit_direction(real_units, head_out, head_in)
    fake_dir = unit_direction(fake_units, head_out, head_in)
    real_cot = (-jax.nn.sigmoid(-margin) * real_dir).astype(jnp.bfloat16)
    fake_cot = (jax.nn.sigmoid(-margin) * fake_dir).astype(jnp.bfloat16)
    gen_cot = (-jax.nn.sigmoid(margin) * fake_dir).astype(jnp.bfloat16)
    head_terms = jnp.einsum("rc,hc->rh", gen_cot, full_out, preferred_element_type=jnp.float32)
    head_grad = lax.psum_scatter(
        head_terms.astype(jnp.bfloat16), "fsdp", scatter_dimension=1, tiled=True
    ).reshape(row_count, head_count, HD)
    scale = HD ** (-0.5)
    slopes = jnp.einsum("rhd,khd->hrk", head_grad, values_two, preferred_element_type=jnp.float32)
    centred = jnp.sum(slopes * second_weights, axis=-1, keepdims=True)
    score_grad = (second_weights * (slopes - centred)).astype(jnp.bfloat16)
    query_grad = (
        jnp.einsum("hrk,khd->rhd", score_grad, keys_two, preferred_element_type=jnp.float32) * scale
    )
    key_part = (
        jnp.einsum("hrk,rhd->khd", score_grad, query_two, preferred_element_type=jnp.float32)
        * scale
    )
    value_part = jnp.einsum(
        "hrk,rhd->khd",
        second_weights.astype(jnp.bfloat16),
        head_grad,
        preferred_element_type=jnp.float32,
    )
    key_grad, value_grad = (
        lax.psum_scatter(
            key_part.reshape(key_count, heads_width).astype(jnp.bfloat16),
            "seq",
            scatter_dimension=0,
            tiled=True,
        ).astype(jnp.float32),
        lax.psum_scatter(
            value_part.reshape(key_count, heads_width).astype(jnp.bfloat16),
            "seq",
            scatter_dimension=0,
            tiled=True,
        ).astype(jnp.float32),
    )
    stacked_grads = jnp.stack(
        [query_grad.reshape(row_count, heads_width), key_grad, value_grad]
    ).astype(jnp.bfloat16)
    row_terms = jnp.einsum(
        "cre,cde->rd", stacked_grads, full_weights, preferred_element_type=jnp.float32
    )
    row_grad = lax.psum_scatter(
        row_terms.astype(jnp.bfloat16), "fsdp", scatter_dimension=1, tiled=True
    ).astype(jnp.float32)
    gain_cols = lax.dynamic_slice_in_dim(gain_vector, start_col, col_count, 0)
    lifted_grad = row_grad * gain_cols
    input_grad = (second_inverse * lifted_grad + gen_cot.astype(jnp.float32)).astype(jnp.bfloat16)
    back_grad, back_pair = passed_along((input_grad, loss_pair), "grp", -1)
    lead_cot = jnp.where(is_gen, back_grad, real_cot)
    tail_cot = jnp.where(is_gen, jnp.zeros_like(fake_cot), fake_cot)
    lead_term = jnp.einsum("rh,rc->hc", first_all, lead_cot, preferred_element_type=jnp.float32)
    tail_term = jnp.einsum("rh,rc->hc", second_all, tail_cot, preferred_element_type=jnp.float32)
    summed = lax.psum_scatter(
        (lead_term + tail_term).astype(jnp.bfloat16), "seq", scatter_dimension=0, tiled=True
    )
    losses = jnp.where(is_gen, back_pair[0], loss_pair[1])
    return (summed[None], losses[None])


def solution(mesh):
    placed = (
        P("seq", None),
        P(None, None, "fsdp"),
        P(None, None, "fsdp"),
        P(),
        P(None, "seq", None),
        P("seq"),
        P("grp", None, "seq", "fsdp"),
        P("grp", "seq", "fsdp"),
        P("grp", None),
        P("fsdp", None),
        P(),
    )
    return jax.shard_map(
        local,
        mesh=mesh,
        in_specs=placed,
        out_specs=(P("grp", "seq", "fsdp"), P("grp")),
        check_vma=False,
    )
```

profile of v0, /device:TPU:0, one launch (start us, length us, event | category | flops | bytes accessed | tf_op | source)
XLA Modules:
  0.0 2044.8 jit_solution(11891159550169487561)
XLA Ops:
  11.1 894.4 %all-gather.16.cloned.1.call-done = bf16[1,3,5120,1536]{3,2,1,0:T(8,128)(2,1)} async-done(((bf16[1,3,640,1536]{3,2,1,0:T(8,128)(2,1)}), bf16[1,3,5120,1536]{3,2,1,0:T(8,128)(2,1)}) %all-gather.16.cloned.1.call-update) | async-done | bytes 47185936 | tf_op jit(solution)/shard_map/all_gather | solution.py:79
  905.6 17.9 fusion.79
  926.1 58.5 %all-gather.18.cloned.1.call-done = bf16[1,1024,1536]{2,1,0:T(8,128)(2,1)} async-done(((bf16[1,128,1536]{2,1,0:T(8,128)(2,1)}), bf16[1,1024,1536]{2,1,0:T(8,128)(2,1)}) %all-gather.18.cloned.1.call-update) | async-done | bytes 3145744 | tf_op jit(solution)/shard_map/all_gather | solution.py:85
  989.2 56.9 %all-gather.20.cloned.1.call-done = bf16[1,1024,1536]{2,1,0:T(8,128)(2,1)} async-done(((bf16[1,128,1536]{2,1,0:T(8,128)(2,1)}), bf16[1,1024,1536]{2,1,0:T(8,128)(2,1)}) %all-gather.20.cloned.1.call-update) | async-done | bytes 3145744 | tf_op jit(solution)/shard_map/all_gather | solution.py:86
  1050.7 102.9 %conditional.2 = (bf16[128,12,128]{0,2,1:T(8,128)(2,1)S(1)}) conditional(s32[]{:T(128)} %convert_element_type.127, (bf16[128,12,128]{0,2,1:T(8,128)(2,1)S(1)}, bf16[1024,12,128]{0,2,1:T(8,128)(2,1)}, bf16[1024,12,128]{0,2,1:T(8,128)(2,1)}) %tuple.72, (bf16[4,512,1536]{2,1,0:T(8,128)(2,1)}, s32[3]{0:T(128)S(1)}, bf16[1024,12,128]{0,2,1:T(8,128)(2,1)}, ...), branch_computations={%region_1.4_spmd, %region_4.8_spmd} | conditional | flops 2081043968 | bytes 162161760
  1092.8 11.1 fusion.16
  1104.1 20.9 %fusion.193 = (f32[12,128]{1,0:T(8,128)S(1)}, f32[12,128,2560]{1,2,0:T(8,128)}) fusion(f32[12,2560,128]{2,1,0:T(8,128)} %fusion.16, pred[128,2560]{0,1:T(8,128)(4,1)S(1)} %concatenate.7), kind=kOutput, calls=%fused_computation.202 | output fusion | flops 23595520 | bytes 31791104 | tf_op jit(solution)/shard_map/cond/branch_1_fun/sub | solution.py:27
  1143.3 10.1 fusion.23
  1162.1 99.2 %all-gather.22.cloned.1.call-done = bf16[1,3072,2560]{2,1,0:T(8,128)(2,1)} async-done(((bf16[1,384,2560]{2,1,0:T(8,128)(2,1)}), bf16[1,3072,2560]{2,1,0:T(8,128)(2,1)}) %all-gather.22.cloned.1.call-update) | async-done | bytes 15728656 | tf_op jit(solution)/shard_map/all_gather | solution.py:80
  1269.9 22.5 %all-gather.14.cloned.1.call-done = bf16[128,5120]{1,0:T(8,128)(2,1)} async-done(((bf16[128,2560]{1,0:T(8,128)(2,1)}), bf16[128,5120]{1,0:T(8,128)(2,1)}) %all-gather.14.cloned.1.call-update) | async-done | bytes 1310736 | tf_op jit(solution)/shard_map/all_gather | solution.py:123
  1297.2 17.9 fusion.76
  1321.1 55.2 %all-gather.24.cloned.1.call-done = bf16[1,1024,1536]{2,1,0:T(8,128)(2,1)} async-done(((bf16[1,128,1536]{2,1,0:T(8,128)(2,1)}), bf16[1,1024,1536]{2,1,0:T(8,128)(2,1)}) %all-gather.24.cloned.1.call-update) | async-done | bytes 3145744 | tf_op jit(solution)/shard_map/all_gather | solution.py:127
  1387.8 49.4 %all-gather.26.cloned.1.call-done = bf16[1,1024,1536]{2,1,0:T(8,128)(2,1)} async-done(((bf16[1,128,1536]{2,1,0:T(8,128)(2,1)}), bf16[1,1024,1536]{2,1,0:T(8,128)(2,1)}) %all-gather.26.cloned.1.call-update) | async-done | bytes 3145744 | tf_op jit(solution)/shard_map/all_gather | solution.py:128
  1465.7 21.2 %all-reduce.5.cloned.1.call-done = (bf16[128,128]{1,0:T(8,128)(2,1)}, bf16[128,128]{1,0:T(8,128)(2,1)}) async-done(((bf16[128,128]{1,0:T(8,128)(2,1)}, bf16[128,128]{1,0:T(8,128)(2,1)}), (bf16[128,128]{1,0:T(8,128)(2,1)}, bf16[128,128]{1,0:T(8,128)(2,1)})) %all-reduce.5.cloned.1.call-update) | async-done | bytes 65552 | tf_op jit(solution)/shard_map/psum | solution.py:143
  1488.3 22.0 %all-reduce.1 = (f32[]{:T(128)}, f32[]{:T(128)}) all-reduce(f32[]{:T(128)} %get-tuple-element.75, f32[]{:T(128)} %get-tuple-element.74), channel_id=1, replica_groups=mesh['grp'=2,'seq'=8,'fsdp'=2] {'seq'}, use_global_device_ids=true, to_apply=%region_12.14 | all-reduce | flops 2 | bytes 16 | tf_op jit(solution)/shard_map/psum | solution.py:147
  1512.8 11.5 fusion.62
  1524.4 13.9 reduce-scatter.10.cloned.1.call-done
  1568.0 59.9 %reduce-scatter.16.cloned.1.call-done = bf16[128,1536]{1,0:T(8,128)(2,1)} async-done(((bf16[1024,1536]{1,0:T(8,128)(2,1)}), bf16[128,1536]{1,0:T(8,128)(2,1)}) %reduce-scatter.16.cloned.1.call-update) | async-done | bytes 393232 | tf_op jit(solution)/shard_map/reduce_scatter | solution.py:177
  1627.9 77.3 %reduce-scatter.18.cloned.1.call-done = bf16[128,1536]{1,0:T(8,128)(2,1)} async-done(((bf16[1024,1536]{1,0:T(8,128)(2,1)}), bf16[128,1536]{1,0:T(8,128)(2,1)}) %reduce-scatter.18.cloned.1.call-update) | async-done | bytes 393232 | tf_op jit(solution)/shard_map/reduce_scatter | solution.py:183
  1705.3 21.4 %fusion.49 = bf16[128,5120]{1,0:T(8,128)(2,1)} fusion(bf16[1,3,5120,1536]{3,2,1,0:T(8,128)(2,1)} %all-gather.16.cloned.1.call-done, bf16[1,128,1536]{2,1,0:T(8,128)(2,1)} %bitcast.154, bf16[1,128,1536]{2,1,0:T(8,128)(2,1)} %bitcast.153, bf16[1,128,1536]{2,1,0:T(8,128)(2,1)S(1)} %copy.75), kind=kOutput, calls=%fused_computation.69 | convolution fusion | flops 6041632768 | bytes 49676288 | tf_op jit(solution)/shard_map/cre,cde->rd/dot_general | solution.py:193
  1726.9 22.4 %reduce-scatter.12.cloned.1.call-done = bf16[128,2560]{1,0:T(8,128)(2,1)} async-done(((bf16[128,5120]{1,0:T(8,128)(2,1)}), bf16[128,2560]{1,0:T(8,128)(2,1)}) %reduce-scatter.12.cloned.1.call-update) | async-done | bytes 655376 | tf_op jit(solution)/shard_map/reduce_scatter | solution.py:196
  1752.9 12.6 fusion.110
  1765.5 18.3 add_convert_fusion
  1787.8 248.9 %reduce-scatter.14.cloned.1.call-done = bf16[384,2560]{1,0:T(8,128)(2,1)} async-done(((bf16[3072,2560]{1,0:T(8,128)(2,1)}), bf16[384,2560]{1,0:T(8,128)(2,1)}) %reduce-scatter.14.cloned.1.call-update) | async-done | bytes 1966096 | tf_op jit(solution)/shard_map/reduce_scatter | solution.py:207
  (116 shorter events, 183.7 us)
Async XLA Ops:
  7.2 1309.7 %copy-start = (bf16[2560,128]{1,0:T(8,128)(2,1)S(1)}, bf16[2560,128]{1,0:T(8,128)(2,1)}, u32[]{:S(2)}) copy-start(bf16[2560,128]{1,0:T(8,128)(2,1)} %param.24) | copy-start | bytes 1966084
  7.2 898.4 %all-gather.16.cloned.1.call-start = ((), (), s32[]{:S(2)}) async-start(), calls=%async_computation.9 | async-start | bytes 53084160 | tf_op jit(solution)/shard_map/all_gather | solution.py:79
  7.9 897.6 %copy-start.6 = (f32[1,5120]{1,0:T(1,128)S(1)}, f32[1,5120]{1,0:T(1,128)}, u32[]{:S(2)}) copy-start(f32[1,5120]{1,0:T(1,128)} %param.23) | copy-start | bytes 61444
  7.9 976.7 %all-gather.18.cloned.1.call-start = ((), (), s32[]{:S(2)}) async-start(), calls=%async_computation.10 | async-start | bytes 3538944 | tf_op jit(solution)/shard_map/all_gather | solution.py:85
  924.5 121.6 %all-gather.20.cloned.1.call-start = ((), (), s32[]{:S(2)}) async-start(), calls=%async_computation.11 | async-start | bytes 3538944 | tf_op jit(solution)/shard_map/all_gather | solution.py:86
  925.2 336.1 %all-gather.22.cloned.1.call-start = ((), (), s32[]{:S(2)}) async-start(), calls=%async_computation.12 | async-start | bytes 17694720 | tf_op jit(solution)/shard_map/all_gather | solution.py:80
  925.8 366.7 %all-gather.14.cloned.1.call-start = ((), (), s32[]{:S(2)}) async-start(), calls=%async_computation.5 | async-start | bytes 1966080 | tf_op jit(solution)/shard_map/all_gather | solution.py:123
  989.2 61.5 %copy-start.13 = (s32[3]{0:T(128)S(1)}, s32[3]{0:T(128)}, u32[]{:S(2)}) copy-start(s32[3]{0:T(128)} %param.18) | copy-start | bytes 40
  1162.1 107.8 %copy-start.2 = (bf16[128,3072]{0,1:T(8,128)(2,1)}, bf16[128,3072]{0,1:T(8,128)(2,1)S(1)}, u32[]{:S(2)}) copy-start(bf16[128,3072]{0,1:T(8,128)(2,1)S(1)} %all_gather.30) | copy-start | bytes 2359300
  1162.1 135.1 %copy-start.7 = (f32[1,5120]{1,0:T(1,128)S(1)}, f32[1,5120]{1,0:T(1,128)}, u32[]{:S(2)}) copy-start(f32[1,5120]{1,0:T(1,128)} %param.23) | copy-start | bytes 61444
  1269.9 106.4 %all-gather.24.cloned.1.call-start = ((), (), s32[]{:S(2)}) async-start(), calls=%async_computation.13 | async-start | bytes 3538944 | tf_op jit(solution)/shard_map/all_gather | solution.py:127
  1292.4 4.4 collective-permute-start
  1316.1 121.1 %all-gather.26.cloned.1.call-start = ((), (), s32[]{:S(2)}) async-start(), calls=%async_computation.14 | async-start | bytes 3538944 | tf_op jit(solution)/shard_map/all_gather | solution.py:128
  1316.9 170.0 %all-reduce.5.cloned.1.call-start = ((), (), s32[]{:S(2)}) async-start(), calls=%async_computation.17 | async-start | bytes 131072 | tf_op jit(solution)/shard_map/psum | solution.py:143
  1319.2 61.8 %copy-start.4 = (bf16[1,128,1536]{1,2,0:T(8,128)(2,1)}, bf16[1,128,1536]{1,2,0:T(8,128)(2,1)S(1)}, u32[]{:S(2)}) copy-start(bf16[1,128,1536]{1,2,0:T(8,128)(2,1)S(1)} %copy.66) | copy-start | bytes 1179652
  1465.6 72.7 %reduce-scatter.10.cloned.1.call-start = ((), (), s32[]{:S(2)}) async-start(), calls=%async_computation.6 | async-start | bytes 1179648 | tf_op jit(solution)/shard_map/reduce_scatter | solution.py:156
  1465.7 58.6 %copy-start.10 = (f32[128]{0:T(128)}, f32[128]{0:T(128)S(1)}, u32[]{:S(2)}) copy-start(f32[128]{0:T(128)S(1)} %broadcast_multiply_fusion) | copy-start | bytes 1540
  1524.3 103.6 %reduce-scatter.16.cloned.1.call-start = ((), (), s32[]{:S(2)}) async-start(), calls=%async_computation.15 | async-start | bytes 3538944 | tf_op jit(solution)/shard_map/reduce_scatter | solution.py:177
  1553.4 151.8 %reduce-scatter.18.cloned.1.call-start = ((), (), s32[]{:S(2)}) async-start(), calls=%async_computation.16 | async-start | bytes 3538944 | tf_op jit(solution)/shard_map/reduce_scatter | solution.py:183
  1563.7 185.6 %reduce-scatter.12.cloned.1.call-start = ((), (), s32[]{:S(2)}) async-start(), calls=%async_computation.7 | async-start | bytes 1966080 | tf_op jit(solution)/shard_map/reduce_scatter | solution.py:196
  1705.2 21.5 %copy-start.8 = (f32[1,5120]{1,0:T(1,128)S(1)}, f32[1,5120]{1,0:T(1,128)}, u32[]{:S(2)}) copy-start(f32[1,5120]{1,0:T(1,128)} %param.23) | copy-start | bytes 61444
  1726.7 310.0 %reduce-scatter.14.cloned.1.call-start = ((), (), s32[]{:S(2)}) async-start(), calls=%async_computation.8 | async-start | bytes 17694720 | tf_op jit(solution)/shard_map/reduce_scatter | solution.py:207
  1751.5 14.0 collective-permute-start.1
  1784.1 3.7 collective-permute-start.2
  (8 other events, 52.3 us)
Sparse Core Ops, SparseCore 0:
  9.5 895.9 all-gather.15
  924.6 59.9 all-gather.17
  987.4 58.6 all-gather.19
  1048.1 213.1 all-gather.21
  1270.0 22.3 all-gather.13
  1316.2 60.0 all-gather.23
  1378.5 58.6 all-gather.25
  1465.7 21.1 all-reduce.4
  1524.4 13.8 reduce-scatter.9
  1553.5 74.3 reduce-scatter.15
  1631.5 73.6 reduce-scatter.17
  1726.8 22.4 reduce-scatter.11
  1783.9 252.7 reduce-scatter.13
where the time goes:
time: 2050 us; the launch traced here: 2040 us
  waiting for transfers between devices  1690 us (82%)
  matrix products  170 us (8%)
  local copies, waits for them, and re-layouts  84.2 us (4%)
  blocking collectives  40.4 us (2%)
  other arithmetic  39.6 us (2%)
    all_gather x1, waiting for transfers between devices, local(): full_weights = lax.all_gather(local_weights, 'seq', axis=1, tiled=True)  894 us
    reduce_scatter x1, waiting for transfers between devices, local(): lax.psum_scatter((lead_term + tail_term).astype(jnp.bfloat16), 'seq', sca...  249 us
    all_gather x1, waiting for transfers between devices, local(): full_out = lax.all_gather(local_out, 'seq', axis=0, tiled=True)  99.2 us
    reduce_scatter x1, waiting for transfers between devices, local(): lax.psum_scatter(value_part.reshape(key_count, heads_width).astype(jnp.bf...  77.3 us
    reduce_scatter x1, waiting for transfers between devices, local(): lax.psum_scatter(key_part.reshape(key_count, heads_width).astype(jnp.bflo...  59.9 us
    all_gather x1, waiting for transfers between devices, local(): lax.all_gather(first_proj[1], 'seq', axis=0, tiled=True)  58.5 us
    all_gather x1, waiting for transfers between devices, local(): lax.all_gather(first_proj[2], 'seq', axis=0, tiled=True)  56.9 us
    all_gather x1, waiting for transfers between devices, local(): lax.all_gather(second_proj[1], 'seq', axis=0, tiled=True)  55.2 us
  transfers between devices with their start and end apart: 16, of which 15 were waited for; matrix products, arithmetic and copies ran while one was open for 8% of the time, Pallas kernels for 0%

commit v1 on v0

v1 whole, which is shorter than its diff:
```python
import functools

import jax
import jax.numpy as jnp
from jax import lax
from jax.experimental import pallas as pl
from jax.experimental.pallas import tpu as pltpu
from jax.sharding import PartitionSpec as P

HD = 128


EPS = 1e-06
NEG = -1e30


def passed_along(value, axis, steps):
    count = lax.axis_size(axis)
    leading, last = (max(0, -steps), min(count, count - steps))
    return lax.ppermute(value, axis, [(source, source + steps) for source in range(leading, last)])


def attend(queries, key_set, value_set, allowed):
    head_size = queries.shape[-1]
    scores = jnp.einsum(
        "rhd,khd->hrk", queries, key_set, preferred_element_type=jnp.float32
    ) * head_size ** (-0.5)
    if allowed is not None:
        scores = jnp.where(allowed[None], scores, NEG)
    row_max = jnp.max(scores, axis=-1, keepdims=True)
    raised = jnp.exp(scores - row_max)
    weights = raised / jnp.sum(raised, axis=-1, keepdims=True)
    result = jnp.einsum(
        "hrk,khd->rhd", weights.astype(jnp.bfloat16), value_set, preferred_element_type=jnp.float32
    )
    return (result, weights)


PIECES = 4


def ring_kernel(count, parts, total, held, send_sems, recv_sems):
    me = lax.axis_index("seq")
    place = (1 - me % 2) * (me // 2) + (me % 2) * (count - 1 - me // 2)

    def device_at(position):
        wrapped = (position + 2 * count) % count
        upper = wrapped // (count // 2)
        return (1 - upper) * 2 * wrapped + upper * (2 * (count - 1 - wrapped) + 1)

    right, left = device_at(place + 1), device_at(place - 1)
    barrier = pltpu.get_barrier_semaphore()
    for neighbour in (left, right):
        pl.semaphore_signal(
            barrier,
            inc=1,
            device_id={"seq": neighbour},
            device_id_type=pl.DeviceIdType.MESH,
        )
    pl.semaphore_wait(barrier, 2)
    rows = total.shape[0] // PIECES
    flying = []
    for step in range(count):
        for piece in range(PIECES):
            forward = piece % 2 == 0
            sign = 1 if forward else -1
            span = pl.ds(piece * rows, rows)
            chunk = device_at(place - sign * (step + 1))
            if step == 0:
                source = parts.at[chunk, span, :]
            else:
                flying[(step - 1) * PIECES + piece].wait_recv()
                own = parts[chunk, span, :].astype(jnp.float32)
                added = held[step - 1, span, :].astype(jnp.float32) + own
                if step == count - 1:
                    total[span, :] = added.astype(total.dtype)
                    continue
                held[step - 1, span, :] = added.astype(held.dtype)
                source = held.at[step - 1, span, :]
            copy = pltpu.make_async_remote_copy(
                src_ref=source,
                dst_ref=held.at[step, span, :],
                send_sem=send_sems.at[step, piece],
                recv_sem=recv_sems.at[step, piece],
                device_id={"seq": right if forward else left},
                device_id_type=pl.DeviceIdType.MESH,
            )
            copy.start()
            flying.append(copy)
    for copy in flying:
        copy.wait_send()


def ring_sum(parts, collective_id):
    count, rows, cols = parts.shape
    return pl.pallas_call(
        functools.partial(ring_kernel, count),
        out_shape=jax.ShapeDtypeStruct((rows, cols), parts.dtype),
        in_specs=[pl.BlockSpec(memory_space=pltpu.VMEM)],
        out_specs=pl.BlockSpec(memory_space=pltpu.VMEM),
        scratch_shapes=[
            pltpu.VMEM((count - 1, rows, cols), parts.dtype),
            pltpu.SemaphoreType.DMA((count - 1, PIECES)),
            pltpu.SemaphoreType.DMA((count - 1, PIECES)),
        ],
        compiler_params=pltpu.CompilerParams(
            collective_id=collective_id, has_side_effects=True, vmem_limit_bytes=60 * 2**20
        ),
    )(parts)


def normalise(row_block, gain_vector):
    lifted = row_block.astype(jnp.float32)
    inverse = lax.rsqrt(jnp.mean(lifted * lifted, axis=-1, keepdims=True) + EPS)
    return ((lifted * inverse * gain_vector).astype(jnp.bfloat16), inverse)


def project(normed, weight_set, deal, kinds, collective_id):
    columns = lax.all_to_all(normed, "seq", 1, 0, tiled=True)
    span = deal * HD
    projected = []
    for member, kind in enumerate(kinds):
        weights = weight_set[:, :, member * span : (member + 1) * span]
        parts = jnp.einsum("td,sdx->stx", columns, weights, preferred_element_type=jnp.float32)
        total = ring_sum(parts.astype(kind), collective_id + member).astype(jnp.bfloat16)
        projected.append(total.reshape(total.shape[0], deal, HD))
    return projected


def unit_gradient(unit_values, head_out):
    _, gelu_back = jax.vjp(jax.nn.gelu, unit_values)
    return gelu_back(jnp.broadcast_to(head_out, unit_values.shape))[0].astype(jnp.bfloat16)


def direction(unit_grad, head_cols):
    return jnp.einsum("tu,cu->tc", unit_grad, head_cols, preferred_element_type=jnp.float32)


def pick_rows(real_bank, real_pick):
    chosen = jnp.zeros(real_bank.shape[1:], real_bank.dtype)
    for entry in range(real_bank.shape[0]):
        chosen = jnp.where((real_pick == entry)[:, None], real_bank[entry], chosen)
    return chosen


def local(
    new_rows,
    cache_keys,
    cache_values,
    cache_frames,
    real_bank,
    real_pick,
    attn_weights,
    out_weights,
    norm_gains,
    head_in,
    head_out,
):
    is_gen = lax.axis_index("grp") == 0
    grp_at = lax.axis_index("grp")
    seq_at = lax.axis_index("seq")
    fsdp_at = lax.axis_index("fsdp")
    seq_n = lax.axis_size("seq")
    grp_n = lax.axis_size("grp")
    row_count, width = new_rows.shape
    token_count = row_count * seq_n
    frame_len = token_count // 2
    own_weights = attn_weights[0]
    own_out = out_weights[0]
    col_count = own_out.shape[1]
    depth = own_weights.shape[1]
    heads_width = own_weights.shape[2]
    head_count = heads_width // HD
    start_col = fsdp_at * col_count
    half = col_count // grp_n
    chunk_at = start_col + grp_at * half

    deal_one = -(-head_count // seq_n)
    deal_two = -(-head_count // (seq_n * grp_n))

    def dealt(count):
        return jnp.pad(own_weights, ((0, 0), (0, 0), (0, count * HD - heads_width)))

    weights_one = (
        dealt(deal_one * seq_n)
        .reshape(3, depth, seq_n, deal_one * HD)
        .transpose(2, 1, 0, 3)
        .reshape(seq_n, depth, 3 * deal_one * HD)
    )
    weights_pair = (
        dealt(deal_two * seq_n * grp_n)
        .reshape(3, depth, seq_n, grp_n, deal_two * HD)
        .transpose(3, 2, 1, 0, 4)
        .reshape(grp_n, seq_n, depth, 3 * deal_two * HD)
    )
    critic_share = passed_along((weights_pair[0], norm_gains[0]), "grp", -1)
    weights_two = jnp.where(is_gen, critic_share[0], weights_pair[1])
    critic_gain = jnp.where(is_gen, critic_share[1], norm_gains[0])

    unit_map = jnp.dot(own_out, head_in, preferred_element_type=jnp.float32)
    unit_map = lax.psum(jnp.where(is_gen, 0.0, unit_map), ("grp", "fsdp"))
    unit_map = lax.all_gather(unit_map, "seq", axis=0, tiled=True)
    unit_map = lax.dynamic_slice_in_dim(unit_map, fsdp_at * heads_width, heads_width, 0)

    def own_map(count, deal, place):
        padded = jnp.pad(unit_map, ((0, count * HD - heads_width), (0, 0)))
        return lax.dynamic_slice_in_dim(padded, place * deal * HD, deal * HD, 0)

    map_one = own_map(deal_one * seq_n, deal_one, seq_at)
    map_two = own_map(deal_two * seq_n * grp_n, deal_two, seq_at * grp_n + grp_at)

    def clip_units(rows, heads, rows_map):
        cols = lax.dynamic_slice_in_dim(rows, start_col, col_count, 1)
        direct = jnp.dot(cols, head_in, preferred_element_type=jnp.float32)
        direct = jnp.where(is_gen, 0.0, direct)
        units = jnp.dot(heads.astype(jnp.float32), rows_map, precision=lax.Precision.HIGHEST)
        spot = lax.dynamic_slice_in_dim(units, seq_at * row_count, row_count, 0)
        return lax.dynamic_update_slice_in_dim(units, spot + direct, seq_at * row_count, 0)

    def to_columns(heads, deal):
        own_tokens = lax.all_to_all(heads, "seq", 0, 1, tiled=True)[:, :heads_width]
        whole = lax.all_gather(own_tokens, "fsdp", axis=1, tiled=True)
        return lax.all_to_all(whole, "seq", 1, 0, tiled=True)

    real_rows = pick_rows(real_bank, real_pick)
    first_rows = jnp.where(is_gen, new_rows, real_rows)
    normed, _ = normalise(first_rows, norm_gains[0])
    query_one, keys_one, values_one = project(normed, weights_one, deal_one, (jnp.float32,) * 3, 1)

    def generator_attend(operand):
        first = jnp.minimum(seq_at * deal_one, head_count - deal_one) * HD

        def picked(cache):
            mine = lax.dynamic_slice_in_dim(cache, first, deal_one * HD, 2)
            return jnp.take(mine, cache_frames, axis=0).reshape(-1, deal_one, HD)

        picked_keys = picked(cache_keys)
        picked_values = picked(cache_values)
        token_frame = jnp.arange(token_count) // frame_len
        allowed = jnp.concatenate(
            [
                jnp.ones((token_count, picked_keys.shape[0]), jnp.bool_),
                token_frame[None, :] <= token_frame[:, None],
            ],
            axis=1,
        )
        all_keys = jnp.concatenate([picked_keys, keys_one], axis=0)
        all_values = jnp.concatenate([picked_values, values_one], axis=0)
        return attend(query_one, all_keys, all_values, allowed)[0].astype(jnp.bfloat16)

    def critic_attend(operand):
        return attend(query_one, keys_one, values_one, None)[0].astype(jnp.bfloat16)

    first_heads = lax.cond(is_gen, generator_attend, critic_attend, 0).reshape(
        token_count, deal_one * HD
    )
    first_cols = to_columns(first_heads, deal_one)
    part = jnp.dot(first_cols, own_out, preferred_element_type=jnp.float32)
    shared = passed_along(part[:, half:], "grp", 1)
    part = jnp.where(is_gen, part[:, :half], shared)
    summed = ring_sum(part.reshape(seq_n, row_count, half), 7)
    chunk = lax.dynamic_slice_in_dim(new_rows, chunk_at, half, 1).astype(jnp.float32)
    chunk = (chunk + summed).astype(jnp.bfloat16)
    generated = lax.all_gather(chunk, ("fsdp", "grp"), axis=1, tiled=True)

    real_units = clip_units(real_rows, first_heads, map_one)
    real_units = lax.psum(jnp.where(is_gen, 0.0, real_units), ("grp", "seq", "fsdp"))
    generated, real_units = lax.optimization_barrier((generated, real_units))

    normed, inverse = normalise(generated, critic_gain)
    query_two, keys_two, values_two = project(
        normed, weights_two, deal_two, (jnp.float32, jnp.float32, jnp.bfloat16), 4
    )
    second_result, second_weights = attend(query_two, keys_two, values_two, None)
    second_heads = second_result.astype(jnp.bfloat16).reshape(token_count, deal_two * HD)
    fake_units = clip_units(generated, second_heads, map_two)
    fake_units = lax.psum(fake_units, ("grp", "seq", "fsdp"))
    paired = lax.all_gather(second_heads, "grp", axis=1, tiled=True)
    second_cols = to_columns(paired, deal_two * grp_n)

    real_score = jnp.sum(jax.nn.gelu(real_units) * head_out)
    fake_score = jnp.sum(jax.nn.gelu(fake_units) * head_out)
    margin = (real_score - fake_score) / token_count
    losses = jnp.where(is_gen, jax.nn.softplus(margin), jax.nn.softplus(-margin))
    real_grad = unit_gradient(real_units, head_out)
    fake_grad = unit_gradient(fake_units, head_out)
    gen_scale = -jax.nn.sigmoid(margin)

    head_grad = (
        gen_scale
        * jnp.einsum(
            "tu,hu->th", fake_grad.astype(jnp.float32), map_two, precision=lax.Precision.HIGHEST
        )
    ).astype(jnp.bfloat16)
    head_grad = head_grad.reshape(token_count, deal_two, HD)
    scale = HD ** (-0.5)
    slopes = jnp.einsum("rhd,khd->hrk", head_grad, values_two, preferred_element_type=jnp.float32)
    centred = jnp.sum(slopes * second_weights, axis=-1, keepdims=True)
    score_grad = (second_weights * (slopes - centred)).astype(jnp.bfloat16)
    query_grad = (
        jnp.einsum("hrk,khd->rhd", score_grad, keys_two, preferred_element_type=jnp.float32) * scale
    )
    key_grad = (
        jnp.einsum("hrk,rhd->khd", score_grad, query_two, preferred_element_type=jnp.float32)
        * scale
    )
    value_grad = jnp.einsum(
        "hrk,rhd->khd",
        second_weights.astype(jnp.bfloat16),
        head_grad,
        preferred_element_type=jnp.float32,
    )
    stacked = jnp.stack([query_grad, key_grad, value_grad], axis=1).astype(jnp.bfloat16)
    stacked = lax.all_gather(
        stacked.reshape(token_count, 3 * deal_two * HD), "seq", axis=0, tiled=False
    )
    critic_scale = jax.nn.sigmoid(-margin)
    real_cot = (-critic_scale * direction(real_grad, head_in)).astype(jnp.bfloat16)
    fake_cot = (critic_scale * direction(fake_grad, head_in)).astype(jnp.bfloat16)
    stacked, second_cols, real_cot, fake_cot = lax.optimization_barrier(
        (stacked, second_cols, real_cot, fake_cot)
    )
    row_terms = jnp.einsum(
        "stx,sdx->td", stacked, weights_two, preferred_element_type=jnp.float32
    ).astype(jnp.bfloat16)
    row_terms = lax.all_to_all(row_terms, "seq", 0, 1, tiled=True)
    row_grad = lax.psum_scatter(
        row_terms, ("fsdp", "grp"), scatter_dimension=1, tiled=True
    ).astype(jnp.float32)
    gain_chunk = lax.dynamic_slice_in_dim(critic_gain, chunk_at, half, 0)
    head_chunk = lax.dynamic_slice_in_dim(head_in, grp_at * half, half, 0)
    own_grad = lax.dynamic_slice_in_dim(fake_grad, seq_at * row_count, row_count, 0)
    gen_cot = (gen_scale * direction(own_grad, head_chunk)).astype(jnp.bfloat16)
    input_grad = (inverse * (row_grad * gain_chunk) + gen_cot.astype(jnp.float32)).astype(
        jnp.bfloat16
    )
    input_grad = lax.all_gather(input_grad, "seq", axis=0, tiled=True)
    other_half = passed_along(input_grad, "grp", -1)
    input_grad = jnp.concatenate([input_grad, other_half], axis=1)

    def product(heads, cotangent):
        return jnp.einsum("th,tc->hc", heads, cotangent, preferred_element_type=jnp.float32)

    wo_grad = lax.cond(
        is_gen,
        lambda _: product(first_cols, input_grad).astype(jnp.bfloat16),
        lambda _: (product(first_cols, real_cot) + product(second_cols, fake_cot)).astype(
            jnp.bfloat16
        ),
        0,
    )
    return (wo_grad[None], losses.astype(jnp.bfloat16)[None])


def solution(mesh):
    placed = (
        P("seq", None),
        P(None, None, "fsdp"),
        P(None, None, "fsdp"),
        P(),
        P(None, "seq", None),
        P("seq"),
        P("grp", None, "seq", "fsdp"),
        P("grp", "seq", "fsdp"),
        P("grp", None),
        P("fsdp", None),
        P(),
    )
    return jax.shard_map(
        local,
        mesh=mesh,
        in_specs=placed,
        out_specs=(P("grp", "seq", "fsdp"), P("grp")),
        check_vma=False,
    )
```

time: 2050 us -> 1270 us (0.62)
  waiting for transfers between devices: 1690 us -> 425 us
  Pallas kernels: 0 us -> 433 us
  blocking collectives: 40.4 us -> 117 us
  matrix products: 170 us -> 102 us
  starting transfers between devices: 5.11 us -> 27.4 us
    all_gather x7 -> x4, waiting for transfers between devices: 1240 us -> 149 us  [the longest x1 55.1 us: local(): input_grad = lax.all_gather(input_grad, 'seq', axis=0, tiled=True)]
    pallas_call x0 -> x7, Pallas kernels: none -> 433 us  [ring_sum(): pl.pallas_call(functools.partial(ring_kernel, count), out_shape=jax.Shape...]
    reduce_scatter x5 -> x1, waiting for transfers between devices: 422 us -> 24.6 us  [local(): lax.psum_scatter(row_terms, ('fsdp', 'grp'), scatter_dimension=1, tiled=T...]
    psum x1 -> x3, waiting for transfers between devices: 21.2 us -> 171 us  [the longest x1 127 us: local(): fake_units = lax.psum(fake_units, ('grp', 'seq', 'fsdp'))]
    all_to_all x0 -> x4, blocking collectives: none -> 97.4 us  [the longest x2 45.8 us: to_columns(): own_tokens = lax.all_to_all(heads, 'seq', 0, 1, tiled=True)[:, :heads_width]]
    all_to_all x0 -> x3, waiting for transfers between devices: none -> 67.4 us  [the longest x2 36.8 us: project(): columns = lax.all_to_all(normed, 'seq', 1, 0, tiled=True)]
    dot_general x10 -> x18, matrix products: 120 us -> 70.2 us  [the longest x6 37.4 us: project(): jnp.einsum('td,sdx->stx', columns, weights, preferred_element_type=jnp.fl...]
    psum x1 -> x0, blocking collectives: 22 us -> none  [local(): real_score, fake_score = lax.psum((real_part, fake_part), 'seq')]
  transfers between devices with their start and end apart: 16 -> 15, of which waited for: 15 -> 13; matrix products, arithmetic and copies ran while one was open for 8% -> 7% of each run, Pallas kernels for 0% -> 5%
where the time goes in v1:
time: 1270 us; the launch traced here: 1260 us
  Pallas kernels  433 us (34%)
  waiting for transfers between devices  425 us (33%)
  blocking collectives  117 us (9%)
  matrix products  102 us (8%)
  local copies, waits for them, and re-layouts  100 us (8%)
  other arithmetic  35.9 us (3%)
  starting transfers between devices  27.4 us (2%)
  between operations  18.1 us (1%)
    pallas_call x7, Pallas kernels, ring_sum(): pl.pallas_call(functools.partial(ring_kernel, count), out_shape=jax.Shape...  433 us
    psum x1, waiting for transfers between devices, local(): fake_units = lax.psum(fake_units, ('grp', 'seq', 'fsdp'))  127 us
    all_gather x1, waiting for transfers between devices, local(): input_grad = lax.all_gather(input_grad, 'seq', axis=0, tiled=True)  55.1 us
    all_gather x1, waiting for transfers between devices, local(): unit_map = lax.all_gather(unit_map, 'seq', axis=0, tiled=True)  46.3 us
    all_to_all x2, blocking collectives, to_columns(): own_tokens = lax.all_to_all(heads, 'seq', 0, 1, tiled=True)[:, :heads_width]  45.8 us
    dot_general x6, matrix products, project(): jnp.einsum('td,sdx->stx', columns, weights, preferred_element_type=jnp.fl...  37.4 us
    all_to_all x2, waiting for transfers between devices, project(): columns = lax.all_to_all(normed, 'seq', 1, 0, tiled=True)  36.8 us
    all_to_all x1, blocking collectives, local(): row_terms = lax.all_to_all(row_terms, 'seq', 0, 1, tiled=True)  34.8 us
  transfers between devices with their start and end apart: 15, of which 13 were waited for; matrix products, arithmetic and copies ran while one was open for 7% of the time, Pallas kernels for 5%

profile of v1, /device:TPU:0, one launch (start us, length us, event | category | flops | bytes accessed | tf_op | source)
XLA Modules:
  0.0 1258.2 jit_solution(16993442351500981904)
XLA Ops:
  75.4 85.0 %shard_map.127 = f32[1024,256]{1,0:T(8,128)} custom-call(f32[8,1024,256]{2,1,0:T(8,128)} %convolution_bitcast_fusion.parts), custom_call_target="tpu_custom_call" | custom-call | tf_op jit(solution)/shard_map/pallas_call | solution.py:96
  162.6 86.6 %shard_map.126 = f32[1024,256]{1,0:T(8,128)} custom-call(f32[8,1024,256]{2,1,0:T(8,128)} %convolution_bitcast_fusion.1.parts), custom_call_target="tpu_custom_call" | custom-call | tf_op jit(solution)/shard_map/pallas_call | solution.py:96
  249.2 84.6 %shard_map.125 = f32[1024,256]{1,0:T(8,128)} custom-call(f32[8,1024,256]{2,1,0:T(8,128)} %convolution_bitcast_fusion.2.parts), custom_call_target="tpu_custom_call" | custom-call | tf_op jit(solution)/shard_map/pallas_call | solution.py:96
  336.3 45.1 %conditional.6 = (bf16[1024,2,128]{0,2,1:T(8,128)(2,1)S(1)}) conditional(s32[]{:T(128)} %convert_element_type.132, (bf16[1024,2,128]{2,1,0:T(2,128)(2,1)S(1)}, bf16[1024,2,128]{2,1,0:T(2,128)(2,1)}, bf16[1024,2,128]{2,1,0:T(2,128)(2,1)}) %tuple.28, (s32[]{:T(128)}, bf16[4,512,1536]{2,1,0:T(8,128)(2,1)}, s32[3]{0:T(128)S(1)}, ...), branch_computations={%region_1.4_spmd, %region_4.8_spmd} | conditional | flops 2722901504 | bytes 77099224
  358.2 14.6 %fusion.156 = (f32[2,1024]{1,0:T(2,128)S(1)}, f32[2,1024,2560]{1,2,0:T(8,128)}) fusion(pred[1024,2560]{0,1:T(8,128)(4,1)} %concatenate.12, bf16[1024,2,128]{2,0,1:T(8,128)(2,1)} %copy.106, bf16[1536,2,128]{2,0,1:T(8,128)(2,1)} %copy.95, bf16[1024,2,128]{2,1,0:T(2,128)(2,1)} %copy-done.26), kind=kOutput, calls=%fused_computation.198 | convolution fusion | flops 1365772800 | bytes 25436160 | tf_op jit(solution)/shard_map/cond/branch_1_fun/sub | solution.py:31
  381.6 13.8 %all_to_all.133 = bf16[8,128,256]{1,2,0:T(8,128)(2,1)S(1)} all-to-all(bf16[8,128,256]{1,2,0:T(8,128)(2,1)S(1)} %copy.108), channel_id=1, replica_groups=mesh['grp'=2,'seq'=8,'fsdp'=2] {'seq'}, dimensions={0} | all-to-all | bytes 1048576 | tf_op jit(solution)/shard_map/all_to_all | solution.py:221
  403.8 16.8 %all_to_all.134 = bf16[128,8,384]{0,2,1:T(8,128)(2,1)} all-to-all(bf16[128,8,384]{0,2,1:T(8,128)(2,1)S(1)} %bitcast.187), channel_id=1, replica_groups=mesh['grp'=2,'seq'=8,'fsdp'=2] {'seq'}, dimensions={1} | all-to-all | bytes 1572864 | tf_op jit(solution)/shard_map/all_to_all | solution.py:223
  435.6 31.1 %all-reduce.7.cloned.1.call-done = f32[384,128]{1,0:T(8,128)} async-done(((f32[384,128]{1,0:T(8,128)}), f32[384,128]{1,0:T(8,128)}) %all-reduce.7.cloned.1.call-update) | async-done | bytes 196624 | tf_op jit(solution)/shard_map/psum | solution.py:201
  466.8 46.3 %all-gather.8.cloned.1.call-done = f32[3072,128]{1,0:T(8,128)} async-done(((f32[384,128]{1,0:T(8,128)}), f32[3072,128]{1,0:T(8,128)}) %all-gather.8.cloned.1.call-update) | async-done | bytes 1572880 | tf_op jit(solution)/shard_map/all_gather | solution.py:202
  523.9 59.1 %shard_map.128 = f32[128,1280]{1,0:T(8,128)} custom-call(f32[8,128,1280]{2,1,0:T(8,128)} %bitcast.167), custom_call_target="tpu_custom_call" | custom-call | tf_op jit(solution)/shard_map/pallas_call | solution.py:96
  585.0 13.6 %reshape.219 = bf16[3,640,8,2,128]{4,3,2,1,0:T(2,128)(2,1)} reshape(bf16[3,640,2048]{2,1,0:T(8,128)(2,1)} %copy-done.2) | data formatting | bytes 15728640 | tf_op jit(solution)/shard_map/reshape | solution.py:192
  598.7 20.1 %copy.110 = bf16[3,640,8,2,128]{1,4,0,2,3:T(8,128)(2,1)} copy(bf16[3,640,8,2,128]{4,3,2,1,0:T(2,128)(2,1)} %reshape.219) | data formatting | bytes 15728640 | tf_op jit(solution)/shard_map/reshape | solution.py:192
  647.1 18.6 %all-gather.6.cloned.1.call-done = bf16[128,5120]{1,0:T(8,128)(2,1)} async-done(((bf16[128,1280]{1,0:T(8,128)(2,1)}), bf16[128,5120]{1,0:T(8,128)(2,1)}) %all-gather.6.cloned.1.call-update) | async-done | bytes 1310736 | tf_op jit(solution)/shard_map/all_gather | solution.py:264
  680.5 27.2 %all-to-all-done.3 = bf16[128,8,640]{2,0,1:T(8,128)(2,1)} async-done(((bf16[128,8,640]{2,0,1:T(8,128)(2,1)}), bf16[128,8,640]{2,0,1:T(8,128)(2,1)}, u32[]{:S(2)}, u32[]{:S(2)}) %all-to-all-start.3) | async-done | bytes 1310752 | tf_op jit(solution)/shard_map/all_to_all | solution.py:119
  722.1 30.5 %shard_map.131 = bf16[1024,128]{1,0:T(8,128)(2,1)} custom-call(bf16[8,1024,128]{2,1,0:T(8,128)(2,1)} %convert_bitcast_fusion.parts), custom_call_target="tpu_custom_call" | custom-call | tf_op jit(solution)/shard_map/pallas_call | solution.py:96
  752.6 45.1 %shard_map.130 = f32[1024,128]{1,0:T(8,128)} custom-call(f32[8,1024,128]{2,1,0:T(8,128)} %convolution_bitcast_fusion.3.parts), custom_call_target="tpu_custom_call" | custom-call | tf_op jit(solution)/shard_map/pallas_call | solution.py:96
  797.7 41.9 %shard_map.129 = f32[1024,128]{1,0:T(8,128)} custom-call(f32[8,1024,128]{2,1,0:T(8,128)} %convolution_bitcast_fusion.4.parts), custom_call_target="tpu_custom_call" | custom-call | tf_op jit(solution)/shard_map/pallas_call | solution.py:96
  845.7 127.0 %all-reduce.11.cloned.1.call-done = f32[1024,128]{1,0:T(8,128)} async-done(((f32[1024,128]{1,0:T(8,128)}), f32[1024,128]{1,0:T(8,128)}) %all-reduce.11.cloned.1.call-update) | async-done | bytes 524304 | tf_op jit(solution)/shard_map/psum | solution.py:277
  988.0 32.1 %all_to_all.135 = bf16[8,128,256]{1,2,0:T(8,128)(2,1)S(1)} all-to-all(bf16[8,128,256]{1,2,0:T(8,128)(2,1)S(1)} %copy.116), channel_id=1, replica_groups=mesh['grp'=2,'seq'=8,'fsdp'=2] {'seq'}, dimensions={0} | all-to-all | bytes 1048576 | tf_op jit(solution)/shard_map/all_to_all | solution.py:221
  1042.7 30.7 %all-to-all-done.5 = bf16[128,8,384]{0,2,1:T(8,128)(2,1)S(1)} async-done(((bf16[128,8,384]{0,2,1:T(8,128)(2,1)}), bf16[128,8,384]{0,2,1:T(8,128)(2,1)S(1)}, u32[]{:S(2)}, u32[]{:S(2)}) %all-to-all-start.5) | async-done | bytes 786464 | tf_op jit(solution)/shard_map/all_to_all | solution.py:223
  1074.6 28.9 %all-gather.10.cloned.1.call-done = bf16[8,1024,384]{2,1,0:T(8,128)(2,1)} async-done(((bf16[1,1024,384]{2,1,0:T(8,128)(2,1)}), bf16[8,1024,384]{2,1,0:T(8,128)(2,1)}) %all-gather.10.cloned.1.call-update) | async-done | bytes 6291472 | tf_op jit(solution)/shard_map/all_gather | solution.py:314
  1111.9 34.8 %all_to_all.136 = bf16[8,128,640]{2,1,0:T(8,128)(2,1)S(1)} all-to-all(bf16[8,128,640]{2,1,0:T(8,128)(2,1)S(1)} %bitcast.194), channel_id=1, replica_groups=mesh['grp'=2,'seq'=8,'fsdp'=2] {'seq'}, dimensions={0} | all-to-all | bytes 2621440 | tf_op jit(solution)/shard_map/all_to_all | solution.py:326
  1148.1 24.6 %reduce-scatter.2.cloned.1.call-done = bf16[128,1280]{1,0:T(8,128)(2,1)} async-done(((bf16[128,5120]{1,0:T(8,128)(2,1)}), bf16[128,1280]{1,0:T(8,128)(2,1)}) %reduce-scatter.2.cloned.1.call-update) | async-done | bytes 327696 | tf_op jit(solution)/shard_map/reduce_scatter | solution.py:327
  1174.7 55.1 %all-gather.12.cloned.1.call-done = bf16[1024,1280]{1,0:T(8,128)(2,1)} async-done(((bf16[128,1280]{1,0:T(8,128)(2,1)}), bf16[1024,1280]{1,0:T(8,128)(2,1)}) %all-gather.12.cloned.1.call-update) | async-done | bytes 2621456 | tf_op jit(solution)/shard_map/all_gather | solution.py:337
  (186 shorter events, 277.5 us)
Async XLA Ops:
  7.2 415.0 %copy-start = (bf16[1,384,2560]{2,1,0:T(8,128)(2,1)S(1)}, bf16[1,384,2560]{2,1,0:T(8,128)(2,1)}, u32[]{:S(2)}) copy-start(bf16[1,384,2560]{2,1,0:T(8,128)(2,1)} %param.24) | copy-start | bytes 5898244
  14.0 38.4 %all-to-all-start = ((bf16[128,8,640]{2,0,1:T(8,128)(2,1)}), bf16[128,8,640]{2,0,1:T(8,128)(2,1)}, u32[]{:S(2)}, u32[]{:S(2)}) async-start(bf16[128,8,640]{2,0,1:T(8,128)(2,1)} %bitcast.161), calls=%async_computation | async-start | bytes 2621440 | tf_op jit(solution)/shard_map/all_to_all | solution.py:119
  21.3 445.4 %all-reduce.7.cloned.1.call-start = ((), (), s32[]{:S(2)}) async-start(), calls=%async_computation.9 | async-start | bytes 393216 | tf_op jit(solution)/shard_map/psum | solution.py:201
  249.2 85.9 %copy-start.16 = (f32[1024,256]{1,0:T(8,128)S(1)}, f32[1024,256]{1,0:T(8,128)}, u32[]{:S(2)}) copy-start(f32[1024,256]{1,0:T(8,128)} %shard_map.126) | copy-start | bytes 3145732
  358.2 14.6 %copy-start.24 = (bf16[1536,2,128]{0,2,1:T(8,128)(2,1)S(1)}, bf16[1536,2,128]{0,2,1:T(8,128)(2,1)}, u32[]{:S(2)}) copy-start(bf16[1536,2,128]{0,2,1:T(8,128)(2,1)} %copy.94) | copy-start | bytes 2359300 | tf_op jit(solution)/shard_map/conditional
  381.4 40.7 %copy-start.15 = (bf16[1024,2,128]{0,2,1:T(8,128)(2,1)}, bf16[1024,2,128]{0,2,1:T(8,128)(2,1)S(1)}, u32[]{:S(2)}) copy-start(bf16[1024,2,128]{0,2,1:T(8,128)(2,1)S(1)} %get-tuple-element.139) | copy-start | bytes 1572868
  430.5 87.8 %collective-permute-start.1 = (f32[1024,1280]{1,0:T(8,128)}, f32[1024,1280]{1,0:T(8,128)}, u32[]{:S(2)}, u32[]{:S(2)}) collective-permute-start(f32[1024,1280]{1,0:T(8,128)} %slice.70), channel_id=1, source_target_pairs={{0,16},{1,17},{2,18},{3,19},{4,20},{5,21},{6,22},{7,23},{8,24},{9,... | collective-permute-start | bytes 15728648 | tf_op jit(solution)/shard_map/ppermute | solution.py:20
  435.5 77.6 %all-gather.8.cloned.1.call-start = ((), (), s32[]{:S(2)}) async-start(), calls=%async_computation.10 | async-start | bytes 1769472 | tf_op jit(solution)/shard_map/all_gather | solution.py:202
  466.7 180.4 %all-reduce.9.cloned.1.call-start = ((), (), s32[]{:S(2)}) async-start(), calls=%async_computation.11 | async-start | bytes 1048576 | tf_op jit(solution)/shard_map/psum | solution.py:267
  518.3 147.5 %all-gather.6.cloned.1.call-start = ((), (), s32[]{:S(2)}) async-start(), calls=%async_computation.8 | async-start | bytes 1638400 | tf_op jit(solution)/shard_map/all_gather | solution.py:264
  624.6 51.5 %collective-permute-start = (bf16[8,640,384]{1,2,0:T(8,128)(2,1)}, bf16[8,640,384]{1,2,0:T(8,128)(2,1)}, u32[]{:S(2)}, u32[]{:S(2)}) collective-permute-start(bf16[8,640,384]{1,2,0:T(8,128)(2,1)} %bitcast.26), channel_id=1, source_target_pairs={{16,0},{17,1},{18,2},{19,3},{20,4},{21,5},{22,6},{23,7},{24,8},{25... | collective-permute-start | bytes 11796488 | tf_op jit(solution)/shard_map/ppermute | solution.py:20
  625.9 7.8 collective-permute-start.2
  670.3 37.4 %all-to-all-start.3 = ((bf16[128,8,640]{2,0,1:T(8,128)(2,1)}), bf16[128,8,640]{2,0,1:T(8,128)(2,1)}, u32[]{:S(2)}, u32[]{:S(2)}) async-start(bf16[128,8,640]{2,0,1:T(8,128)(2,1)} %bitcast.177), calls=%async_computation.3 | async-start | bytes 2621440 | tf_op jit(solution)/shard_map/all_to_all | solution.py:119
  675.8 296.9 %all-reduce.11.cloned.1.call-start = ((), (), s32[]{:S(2)}) async-start(), calls=%async_computation.12 | async-start | bytes 1048576 | tf_op jit(solution)/shard_map/psum | solution.py:277
  797.7 41.9 %copy-start.13 = (f32[1024,128]{1,0:T(8,128)S(1)}, f32[1024,128]{1,0:T(8,128)}, u32[]{:S(2)}) copy-start(f32[1024,128]{1,0:T(8,128)} %shard_map.130) | copy-start | bytes 1572868
  845.4 258.2 %all-gather.10.cloned.1.call-start = ((), (), s32[]{:S(2)}) async-start(), calls=%async_computation.13 | async-start | bytes 7077888 | tf_op jit(solution)/shard_map/all_gather | solution.py:314
  985.5 49.4 %copy-start.19 = (bf16[1024,128]{1,0:T(8,128)(2,1)S(1)}, bf16[1024,128]{1,0:T(8,128)(2,1)}, u32[]{:S(2)}) copy-start(bf16[1024,128]{1,0:T(8,128)(2,1)} %copy-done.18) | copy-start | bytes 786436
  1028.6 44.8 %all-to-all-start.5 = ((bf16[128,8,384]{0,2,1:T(8,128)(2,1)}), bf16[128,8,384]{0,2,1:T(8,128)(2,1)S(1)}, u32[]{:S(2)}, u32[]{:S(2)}) async-start(bf16[128,8,384]{0,2,1:T(8,128)(2,1)} %bitcast.185), calls=%async_computation.5 | async-start | bytes 1572864 | tf_op jit(solution)/shard_map/all_to_all | solution.py:223
  1034.7 137.9 %reduce-scatter.2.cloned.1.call-start = ((), (), s32[]{:S(2)}) async-start(), calls=%async_computation.14 | async-start | bytes 1638400 | tf_op jit(solution)/shard_map/reduce_scatter | solution.py:327
  1147.9 81.9 %all-gather.12.cloned.1.call-start = ((), (), s32[]{:S(2)}) async-start(), calls=%async_computation.15 | async-start | bytes 2949120 | tf_op jit(solution)/shard_map/all_gather | solution.py:337
  1172.6 69.5 %copy-start.12 = (bf16[8,128,384]{2,1,0:T(8,128)(2,1)S(1)}, bf16[8,128,384]{2,1,0:T(8,128)(2,1)}, u32[]{:S(2)}) copy-start(bf16[8,128,384]{2,1,0:T(8,128)(2,1)} %copy.117) | copy-start | bytes 2359300
  1229.8 7.1 collective-permute-start.3
  1231.6 10.5 slice-start
  1231.7 10.5 slice-start.1
  (25 other events, 109.7 us)
Sparse Core Ops, SparseCore 0:
  435.6 31.0 all-reduce.6
  468.9 44.1 all-gather.7
  518.9 128.1 all-reduce.8
  648.5 17.1 all-gather.5
  845.5 127.1 all-reduce.10
  985.6 117.9 all-gather.9
  1148.1 24.5 reduce-scatter.1
  1175.4 54.3 all-gather.11
